TPU v7x, 32 devices: a whole 2x2x4 slice. The times are simulated.
32 devices in a mesh: grp: 2 (over y), gz: 4 (over z), gy: 2 (over x), sa: 2 (over core).
Axes of the slice: x: 2, y: 2, z: 4, core: 2. Of those that a mesh axis runs over, the one named last changes fastest.
Arguments:
- field: float32 [8, 32, 16, 128], P('sa', ('grp', 'gz'), 'gy'), parts along dimension 1, may hold values from 0 to 2
- diffusion: float32 [8], P('sa'), may hold values from 0.02 to 0.16
- secrete: float32 [8, 65536], P('sa', ('grp', 'gz', 'gy')), parts along dimension 1, may hold values from 0 to 1
- uptake: float32 [8, 65536], P('sa', ('grp', 'gz', 'gy')), parts along dimension 1, may hold values from 0.05 to 1
- cell_voxel: int32 [65536], P(('grp', 'gz', 'gy')), parts along dimension 0, may hold values from 0 to 4095
- block_dest: int32 [512, 1], P(('grp', 'gz', 'gy')), parts along dimension 0, may hold values from 0 to 3; in each aligned block of 32 rows (0 to 31, 32 to 63, ...) at most 24 rows name the same one
Outputs:
- new_field: float32 [8, 32, 16, 128], P('sa', ('grp', 'gz'), 'gy'), parts along dimension 1
- cell_conc: float32 [8, 65536], P('sa', ('grp', 'gz', 'gy')), parts along dimension 1
There are 2 independent parts, one for each index of `grp`. A program takes and returns all parts, laid end to end along the dimension named above; an argument that names none is the same for every part. Nothing has to cross between parts.
Inputs may be any that keep to these rules, and one draw needn't show every extreme that they name: `block_dest`: among the 32 blocks of one device at most 24 name the same destination, and in every draw some device has exactly 24 blocks naming one destination.
All inputs are finite; a program needn't handle non-finite values.
Results may differ from a plain program's by a relative error of at most 0.00007.
Values sent between devices are 32-bit elements; how exact they have to be, the bound alone decides.
A program may use at most 64 MiB of HBM per device.

v0:
```python
import math
import jax
import jax.numpy as jnp
from jax import lax
from jax.sharding import PartitionSpec as P

HIGH = lax.Precision.HIGHEST


def extended(block, sides, width):
    for axis, dim in sides:
        count = lax.axis_size(axis)
        forward = [(i, i + 1) for i in range(count - 1)]
        backward = [(target, source) for source, target in forward]
        low = lax.ppermute(
            lax.slice_in_dim(block, block.shape[dim] - width, None, axis=dim), axis, forward
        )
        high = lax.ppermute(lax.slice_in_dim(block, 0, width, axis=dim), axis, backward)
        block = jnp.concatenate([low, block, high], axis=dim)
    return block


def neighbours(padded):
    beside_all = padded[:, 2:, 1:-1, 1:-1] + padded[:, :-2, 1:-1, 1:-1]
    beside_all = beside_all + padded[:, 1:-1, 2:, 1:-1] + padded[:, 1:-1, :-2, 1:-1]
    return beside_all + padded[:, 1:-1, 1:-1, 2:] + padded[:, 1:-1, 1:-1, :-2]


def diffuse(field, diffusion):
    padded = extended(field, (("gz", 1), ("gy", 2)), 1)
    padded = jnp.pad(padded, ((0, 0), (0, 0), (0, 0), (1, 1)))
    return field + diffusion[:, None, None, None] * (neighbours(padded) - 6.0 * field)


def group_size(block_count, per_block):
    return math.gcd(block_count, max(1, 512 // per_block))


def one_hots(voxel_group, highs, lanes):
    high_ids = jnp.arange(highs, dtype=jnp.int32)
    lane_ids = jnp.arange(lanes, dtype=jnp.int32)
    onehot_high = ((voxel_group // lanes)[..., None] == high_ids).astype(jnp.float32)
    onehot_low = ((voxel_group % lanes)[..., None] == lane_ids).astype(jnp.float32)
    return (onehot_high, onehot_low)


def block_sums(values, voxel, highs, lanes, combine, init):
    quantities, block_count, per_block = values.shape
    group = group_size(block_count, per_block)
    steps_count = block_count // group
    grouped_vals = values.reshape(quantities, steps_count, group, per_block).transpose(1, 0, 2, 3)
    grouped_vox = voxel.reshape(steps_count, group, per_block)

    def step(carry, item):
        vals_group, vox_group, step_id = item
        onehot_high, onehot_low = one_hots(vox_group, highs, lanes)
        weighted = vals_group[:, :, :, None] * onehot_low[None]
        part = jnp.einsum("gch,qgcl->gqhl", onehot_high, weighted, precision=HIGH)
        return (combine(carry, part, step_id * group, group), None)

    result, unused = lax.scan(
        step, init, (grouped_vals, grouped_vox, jnp.arange(steps_count, dtype=jnp.int32))
    )
    return result


def block_reads(table_for, voxel, substrates, highs, lanes):
    block_count, per_block = voxel.shape
    group = group_size(block_count, per_block)
    steps_count = block_count // group
    grouped_vox = voxel.reshape(steps_count, group, per_block)

    def step(carry, item):
        vox_group, step_id = item
        onehot_high, onehot_low = one_hots(vox_group, highs, lanes)
        table = table_for(step_id * group, group)
        picked = jnp.einsum("gch,shl->gscl", onehot_high, table, precision=HIGH)
        return (carry, jnp.sum(picked * onehot_low[:, None], axis=3))

    unused, reads = lax.scan(step, 0, (grouped_vox, jnp.arange(steps_count, dtype=jnp.int32)))
    return reads.transpose(2, 0, 1, 3).reshape(substrates, block_count, per_block)


def deposit(secrete, uptake, cell_voxel, block_dest, voxels, lanes):
    substrates = secrete.shape[0]
    blocks = block_dest.shape[0]
    per_block = secrete.shape[1] // blocks
    highs = voxels // lanes
    slab_count = lax.axis_size("gz")
    targets = block_dest[:, 0]
    voxel_blocks = cell_voxel.reshape(blocks, per_block)
    capacity = max(2, 3 * blocks // slab_count)
    block_ids = jnp.arange(blocks, dtype=jnp.int32)
    matches = targets[:, None] == targets[None, :]
    earlier = block_ids[None, :] < block_ids[:, None]
    slot_index = jnp.sum((matches & earlier).astype(jnp.int32), axis=1)
    position = targets * capacity + slot_index
    slots = slab_count * capacity
    placing = (jnp.arange(slots, dtype=jnp.int32)[:, None] == position[None, :]).astype(jnp.float32)
    send_release = jnp.einsum(
        "pb,sbc->spc", placing, secrete.reshape(substrates, blocks, per_block), precision=HIGH
    )
    send_uptake = jnp.einsum(
        "pb,sbc->spc", placing, uptake.reshape(substrates, blocks, per_block), precision=HIGH
    )
    send_index = jnp.dot(placing, voxel_blocks.astype(jnp.float32), precision=HIGH)
    send_index = send_index.astype(jnp.int32).reshape(1, slots, per_block)
    got_release, got_uptake, got_index = (
        lax.all_to_all(send_release, "gz", split_axis=1, concat_axis=1, tiled=True),
        lax.all_to_all(send_uptake, "gz", split_axis=1, concat_axis=1, tiled=True),
        lax.all_to_all(send_index, "gz", split_axis=1, concat_axis=1, tiled=True),
    )
    slot_voxel = got_index.reshape(slots, per_block)
    stacked = jnp.concatenate([got_release, got_uptake], axis=0)

    def add_all(carry, part, first, count):
        return carry + jnp.sum(part, axis=0)

    init = jnp.zeros((2 * substrates, highs, lanes), jnp.float32)
    summed = block_sums(stacked, slot_voxel, highs, lanes, add_all, init).reshape(
        2 * substrates, voxels
    )
    source = summed[:substrates]
    uptake_sum = summed[substrates:]

    def reader(updated):
        table = updated.reshape(substrates, highs, lanes)
        looked_up = block_reads(lambda first, count: table, slot_voxel, substrates, highs, lanes)
        returned = lax.all_to_all(looked_up, "gz", split_axis=1, concat_axis=1, tiled=True)
        back = jnp.einsum("pb,spc->sbc", placing, returned, precision=HIGH)
        return back.reshape(substrates, blocks * per_block)

    return (source, uptake_sum, reader)


def shards(field, diffusion, secrete, uptake, cell_voxel, block_dest):
    substrates = field.shape[0]
    lanes = field.shape[3]
    voxels = field.shape[1] * field.shape[2] * lanes
    source, uptake_sum, reader = deposit(secrete, uptake, cell_voxel, block_dest, voxels, lanes)
    diffused = diffuse(field, diffusion).reshape(substrates, voxels)
    updated = (diffused + source) / (1.0 + uptake_sum)
    cell_conc = reader(updated)
    return (updated.reshape(field.shape), cell_conc)


def solution(mesh):
    in_specs = (
        P("sa", ("grp", "gz"), "gy", None),
        P("sa"),
        P("sa", ("grp", "gz", "gy")),
        P("sa", ("grp", "gz", "gy")),
        P(("grp", "gz", "gy")),
        P(("grp", "gz", "gy"), None),
    )
    out_specs = (P("sa", ("grp", "gz"), "gy", None), P("sa", ("grp", "gz", "gy")))
    return jax.shard_map(shards, mesh=mesh, in_specs=in_specs, out_specs=out_specs, check_vma=False)
```

profile of v0, /device:TPU:0, one launch (start us, length us, event | category | flops | bytes accessed | tf_op | source)
XLA Modules:
  0.0 118.7 jit_solution(11826581008800157441)
XLA Ops:
  0.6 0.9 convert_reduce_fusion
  2.2 1.2 %convolution_bitcast_fusion = f32[4,96,128]{2,1,0:T(8,128)S(1)} fusion(f32[1,4,32,128]{3,1,2,0:T(4,128)} %bitcast.137, s32[32]{0:T(128)S(1)} %multiply_add_fusion), kind=kOutput, calls=%fused_computation.41 | convolution fusion | flops 18877440 | bytes 262272 | tf_op jit(solution)/shard_map/pb,sbc->spc/dot_general | solution.py:103
  3.4 0.8 copy.16
  4.2 6.3 %all-to-all-start.1 = ((f32[4,96,128]{2,0,1:T(4,128)}), f32[4,96,128]{2,0,1:T(4,128)S(1)}, u32[]{:S(2)}, u32[]{:S(2)}) async-start(f32[4,96,128]{2,0,1:T(4,128)} %copy.16), calls=%async_computation.1 | async-start | bytes 393216 | tf_op jit(solution)/shard_map/all_to_all | solution.py:110
  10.6 3.9 %collective-permute-start.1 = (f32[4,1,8,128]{3,2,1,0:T(8,128)S(1)}, f32[4,1,8,128]{3,2,1,0:T(8,128)S(1)}, u32[]{:S(2)}, u32[]{:S(2)}) collective-permute-start(f32[4,1,8,128]{3,2,1,0:T(8,128)S(1)} %get-tuple-element.156), channel_id=1, source_target_pairs={{0,4},{4,8},{8,12},{1,5},{5,9},{9,13},{2,6},{6,10},{10,14},{3,7},{... | collective-permute-start | bytes 49160 | tf_op jit(solution)/shard_map/ppermute | solution.py:15
  14.5 1.3 %collective-permute-start = (f32[4,1,8,128]{3,2,1,0:T(8,128)S(1)}, f32[4,1,8,128]{3,2,1,0:T(8,128)S(1)}, u32[]{:S(2)}, u32[]{:S(2)}) collective-permute-start(f32[4,1,8,128]{3,2,1,0:T(8,128)S(1)} %get-tuple-element.155), channel_id=1, source_target_pairs={{4,0},{8,4},{12,8},{5,1},{9,5},{13,9},{6,2},{10,6},{14,10},{7,3},{... | collective-permute-start | bytes 49160 | tf_op jit(solution)/shard_map/ppermute | solution.py:18
  16.2 0.8 copy.15
  17.0 3.1 %collective-permute-done = f32[4,1,8,128]{3,2,1,0:T(8,128)S(1)} collective-permute-done((f32[4,1,8,128]{3,2,1,0:T(8,128)S(1)}, f32[4,1,8,128]{3,2,1,0:T(8,128)S(1)}, u32[]{:S(2)}, u32[]{:S(2)}) %collective-permute-start) | collective-permute-done | bytes 16416 | tf_op jit(solution)/shard_map/ppermute | solution.py:18
  20.2 1.3 %collective-permute-start.2 = (f32[4,6,1,128]{3,2,1,0:T(1,128)S(1)}, f32[4,6,1,128]{3,2,1,0:T(1,128)S(1)}, u32[]{:S(2)}, u32[]{:S(2)}) collective-permute-start(f32[4,6,1,128]{3,2,1,0:T(1,128)S(1)} %get-tuple-element.154), channel_id=1, source_target_pairs={{2,0},{3,1},{6,4},{7,5},{10,8},{11,9},{14,12},{15,13},{18,16},{19,... | collective-permute-start | bytes 36872 | tf_op jit(solution)/shard_map/ppermute | solution.py:18
  21.5 4.5 %collective-permute-start.3 = (f32[4,6,1,128]{3,2,1,0:T(1,128)S(1)}, f32[4,6,1,128]{3,2,1,0:T(1,128)S(1)}, u32[]{:S(2)}, u32[]{:S(2)}) collective-permute-start(f32[4,6,1,128]{3,2,1,0:T(1,128)S(1)} %get-tuple-element.153), channel_id=1, source_target_pairs={{0,2},{1,3},{4,6},{5,7},{8,10},{9,11},{12,14},{13,15},{16,18},{17,... | collective-permute-start | bytes 36872 | tf_op jit(solution)/shard_map/ppermute | solution.py:15
  26.0 3.6 %all-to-all-start = ((f32[4,96,128]{2,0,1:T(4,128)}), f32[4,96,128]{2,0,1:T(4,128)S(1)}, u32[]{:S(2)}, u32[]{:S(2)}) async-start(f32[4,96,128]{2,0,1:T(4,128)} %copy.15), calls=%async_computation | async-start | bytes 393216 | tf_op jit(solution)/shard_map/all_to_all | solution.py:109
  29.7 0.9 convolution_convert_fusion
  30.9 5.0 %all-to-all-done = f32[4,96,128]{2,0,1:T(4,128)S(1)} async-done(((f32[4,96,128]{2,0,1:T(4,128)}), f32[4,96,128]{2,0,1:T(4,128)S(1)}, u32[]{:S(2)}, u32[]{:S(2)}) %all-to-all-start) | async-done | bytes 196640 | tf_op jit(solution)/shard_map/all_to_all | solution.py:109
  35.9 3.3 %all-to-all-start.2 = ((s32[1,96,128]{2,0,1:T(1,128)}), s32[1,96,128]{2,0,1:T(1,128)S(1)}, u32[]{:S(2)}, u32[]{:S(2)}) async-start(s32[1,96,128]{2,0,1:T(1,128)} %bitcast.14), calls=%async_computation.2 | async-start | bytes 98304 | tf_op jit(solution)/shard_map/all_to_all | solution.py:111
  39.4 5.5 %all-to-all-done.2 = s32[1,96,128]{2,0,1:T(1,128)S(1)} async-done(((s32[1,96,128]{2,0,1:T(1,128)}), s32[1,96,128]{2,0,1:T(1,128)S(1)}, u32[]{:S(2)}, u32[]{:S(2)}) %all-to-all-start.2) | async-done | bytes 49184 | tf_op jit(solution)/shard_map/all_to_all | solution.py:111
  44.9 31.3 %while.26 = (s32[]{:T(128)}, f32[8,32,128]{2,1,0:T(8,128)S(1)}, f32[24,8,4,128]{3,2,1,0:T(4,128)S(1)}, s32[24,4,128]{2,1,0:T(4,128)S(1)}, s32[]{:T(128)}, /*index=5*/s32[]{:T(128)}) while((s32[]{:T(128)}, f32[8,32,128]{2,1,0:T(8,128)S(1)}, f32[24,8,4,128]{3,2,1,0:T(4,128)S(1)}, s32[24,4,128]{2,1,0:T(4,128)S(1)}, s32[]{:T(128)}, ...), condition=%wide.region_2.3_spmd.clone, body=%wide.region_1.2_spmd.clone.sunk | while | flops 202073600 | bytes 845919 | solution.py:61
  45.0 1.1 fusion.66
  46.4 1.1 fusion.66
  47.7 1.1 fusion.66
  49.0 1.1 fusion.66
  50.3 1.1 fusion.66
  51.6 1.1 fusion.66
  52.9 1.1 fusion.66
  54.2 1.1 fusion.66
  55.5 1.1 fusion.66
  56.8 1.1 fusion.66
  58.1 1.1 fusion.66
  59.4 1.1 fusion.66
  60.7 1.1 fusion.66
  62.0 1.1 fusion.66
  63.3 1.1 fusion.66
  64.6 1.1 fusion.66
  65.9 1.1 fusion.66
  67.2 1.1 fusion.66
  68.5 1.1 fusion.66
  69.8 1.1 fusion.66
  71.1 1.1 fusion.66
  72.4 1.1 fusion.66
  73.7 1.1 fusion.66
  75.0 1.1 fusion.66
  76.3 31.9 %while.25 = (s32[]{:T(128)}, f32[24,4,4,128]{3,2,1,0:T(4,128)}, s32[24,4,128]{2,1,0:T(4,128)S(1)}, f32[4,32,128]{2,1,0:T(8,128)S(1)}, s32[]{:T(128)}) while((s32[]{:T(128)}, f32[24,4,4,128]{3,2,1,0:T(4,128)}, s32[24,4,128]{2,1,0:T(4,128)S(1)}, f32[4,32,128]{2,1,0:T(8,128)S(1)}, s32[]{:T(128)}) %tuple.72), condition=%wide.region_5.6_spmd, body=%wide.region_3.5_spmd.sunk | while | flops 101342720 | bytes 624717 | solution.py:80
  76.3 0.7 fusion.62
  77.7 0.7 fusion.62
  80.3 0.7 fusion.62
  83.0 0.7 fusion.62
  84.3 0.7 fusion.62
  85.6 0.7 fusion.62
  86.9 0.7 fusion.62
  88.3 0.7 fusion.62
  89.6 0.7 fusion.62
  90.9 0.7 fusion.62
  92.3 0.7 fusion.62
  93.6 0.7 fusion.62
  94.9 0.7 fusion.62
  96.3 0.7 fusion.62
  97.6 0.7 fusion.62
  98.9 0.7 fusion.62
  100.3 0.7 fusion.62
  101.6 0.7 fusion.62
  102.9 0.7 fusion.62
  104.2 0.7 fusion.62
  105.6 0.7 fusion.62
  108.2 3.4 %all-to-all-start.3 = ((f32[4,96,128]{2,0,1:T(4,128)}), f32[4,96,128]{2,0,1:T(4,128)S(1)}, u32[]{:S(2)}, u32[]{:S(2)}) async-start(f32[4,96,128]{2,0,1:T(4,128)} %bitcast.20), calls=%async_computation.3 | async-start | bytes 393216 | tf_op jit(solution)/shard_map/all_to_all | solution.py:129
  112.2 5.6 %all-to-all-done.3 = f32[4,96,128]{2,0,1:T(4,128)S(1)} async-done(((f32[4,96,128]{2,0,1:T(4,128)}), f32[4,96,128]{2,0,1:T(4,128)S(1)}, u32[]{:S(2)}, u32[]{:S(2)}) %all-to-all-start.3) | async-done | bytes 196640 | tf_op jit(solution)/shard_map/all_to_all | solution.py:129
  (175 shorter events, 24.3 us)
Async XLA Ops:
  3.4 7.2 %copy-start = (f32[4,4,8,128]{3,2,1,0:T(8,128)S(1)}, f32[4,4,8,128]{3,2,1,0:T(8,128)}, u32[]{:S(2)}) copy-start(f32[4,4,8,128]{3,2,1,0:T(8,128)} %param.10) | copy-start | bytes 196612
  3.4 12.4 %copy-start.1 = (f32[4,4096]{1,0:T(4,128)S(1)}, f32[4,4096]{1,0:T(4,128)}, u32[]{:S(2)}) copy-start(f32[4,4096]{1,0:T(4,128)} %param.12) | copy-start | bytes 196612
  4.2 21.8 %all-to-all-start.1 = ((f32[4,96,128]{2,0,1:T(4,128)}), f32[4,96,128]{2,0,1:T(4,128)S(1)}, u32[]{:S(2)}, u32[]{:S(2)}) async-start(f32[4,96,128]{2,0,1:T(4,128)} %copy.16), calls=%async_computation.1 | async-start | bytes 393216 | tf_op jit(solution)/shard_map/all_to_all | solution.py:110
  10.6 6.4 %collective-permute-start.1 = (f32[4,1,8,128]{3,2,1,0:T(8,128)S(1)}, f32[4,1,8,128]{3,2,1,0:T(8,128)S(1)}, u32[]{:S(2)}, u32[]{:S(2)}) collective-permute-start(f32[4,1,8,128]{3,2,1,0:T(8,128)S(1)} %get-tuple-element.156), channel_id=1, source_target_pairs={{0,4},{4,8},{8,12},{1,5},{5,9},{9,13},{2,6},{6,10},{10,14},{3,7},{... | collective-permute-start | bytes 49160 | tf_op jit(solution)/shard_map/ppermute | solution.py:15
  14.5 5.6 %collective-permute-start = (f32[4,1,8,128]{3,2,1,0:T(8,128)S(1)}, f32[4,1,8,128]{3,2,1,0:T(8,128)S(1)}, u32[]{:S(2)}, u32[]{:S(2)}) collective-permute-start(f32[4,1,8,128]{3,2,1,0:T(8,128)S(1)} %get-tuple-element.155), channel_id=1, source_target_pairs={{4,0},{8,4},{12,8},{5,1},{9,5},{13,9},{6,2},{10,6},{14,10},{7,3},{... | collective-permute-start | bytes 49160 | tf_op jit(solution)/shard_map/ppermute | solution.py:18
  17.0 12.7 %copy-start.2 = (s32[4096]{0:T(1024)S(1)}, s32[4096]{0:T(1024)}, u32[]{:S(2)}) copy-start(s32[4096]{0:T(1024)} %param.14) | copy-start | bytes 49156
  20.2 10.4 %collective-permute-start.2 = (f32[4,6,1,128]{3,2,1,0:T(1,128)S(1)}, f32[4,6,1,128]{3,2,1,0:T(1,128)S(1)}, u32[]{:S(2)}, u32[]{:S(2)}) collective-permute-start(f32[4,6,1,128]{3,2,1,0:T(1,128)S(1)} %get-tuple-element.154), channel_id=1, source_target_pairs={{2,0},{3,1},{6,4},{7,5},{10,8},{11,9},{14,12},{15,13},{18,16},{19,... | collective-permute-start | bytes 36872 | tf_op jit(solution)/shard_map/ppermute | solution.py:18
  21.5 9.1 %collective-permute-start.3 = (f32[4,6,1,128]{3,2,1,0:T(1,128)S(1)}, f32[4,6,1,128]{3,2,1,0:T(1,128)S(1)}, u32[]{:S(2)}, u32[]{:S(2)}) collective-permute-start(f32[4,6,1,128]{3,2,1,0:T(1,128)S(1)} %get-tuple-element.153), channel_id=1, source_target_pairs={{0,2},{1,3},{4,6},{5,7},{8,10},{9,11},{12,14},{13,15},{16,18},{17,... | collective-permute-start | bytes 36872 | tf_op jit(solution)/shard_map/ppermute | solution.py:15
  26.0 9.9 %all-to-all-start = ((f32[4,96,128]{2,0,1:T(4,128)}), f32[4,96,128]{2,0,1:T(4,128)S(1)}, u32[]{:S(2)}, u32[]{:S(2)}) async-start(f32[4,96,128]{2,0,1:T(4,128)} %copy.15), calls=%async_computation | async-start | bytes 393216 | tf_op jit(solution)/shard_map/all_to_all | solution.py:109
  35.9 8.9 %all-to-all-start.2 = ((s32[1,96,128]{2,0,1:T(1,128)}), s32[1,96,128]{2,0,1:T(1,128)S(1)}, u32[]{:S(2)}, u32[]{:S(2)}) async-start(s32[1,96,128]{2,0,1:T(1,128)} %bitcast.14), calls=%async_computation.2 | async-start | bytes 98304 | tf_op jit(solution)/shard_map/all_to_all | solution.py:111
  44.9 31.3 %copy-start.3 = (f32[4]{0:T(128)S(1)}, f32[4]{0:T(128)}, u32[]{:S(2)}) copy-start(f32[4]{0:T(128)} %param.11) | copy-start | bytes 52
  108.2 9.6 %all-to-all-start.3 = ((f32[4,96,128]{2,0,1:T(4,128)}), f32[4,96,128]{2,0,1:T(4,128)S(1)}, u32[]{:S(2)}, u32[]{:S(2)}) async-start(f32[4,96,128]{2,0,1:T(4,128)} %bitcast.20), calls=%async_computation.3 | async-start | bytes 393216 | tf_op jit(solution)/shard_map/all_to_all | solution.py:129
where the time goes:
time: 119 us
  matrix products  45.3 us (38%)
  starting transfers between devices  27.7 us (23%)
  waiting for transfers between devices  19.2 us (16%)
  local copies, waits for them, and re-layouts  17.1 us (14%)
  other arithmetic  7.06 us (6%)
  loops' own time  1.48 us (1%)
    dot_general x24, matrix products, step(): part = jnp.einsum('gch,qgcl->gqhl', onehot_high, weighted, precision=HIGH)  26.3 us
    dot_general x24, matrix products, step(): picked = jnp.einsum('gch,shl->gscl', onehot_high, table, precision=HIGH)  16.3 us
    dynamic_update_slice x24, local copies, waits for them, and re-layouts, block_reads(): lax.scan(step, 0, (grouped_vox, jnp.arange(steps_count, dtype=jnp.int32)))  14.4 us
    ppermute x2, starting transfers between devices, extended(): lax.ppermute(lax.slice_in_dim(block, block.shape[dim] - width, None, axis...  8.46 us
    all_to_all x1, starting transfers between devices, deposit(): lax.all_to_all(send_uptake, 'gz', split_axis=1, concat_axis=1, tiled=True)  6.35 us
    all_to_all x1, waiting for transfers between devices, reader(): lax.all_to_all(looked_up, 'gz', split_axis=1, concat_axis=1, tiled=True)  5.57 us
    all_to_all x1, waiting for transfers between devices, deposit(): lax.all_to_all(send_index, 'gz', split_axis=1, concat_axis=1, tiled=True)  5.47 us
    all_to_all x1, waiting for transfers between devices, deposit(): lax.all_to_all(send_release, 'gz', split_axis=1, concat_axis=1, tiled=True)  5.03 us
  transfers between devices with their start and end apart: 8, of which 4 were waited for; matrix products, arithmetic and copies ran while one was open for 3% of the time, Pallas kernels for 0%

commit v1 on v0

--- a/solution.py
+++ b/solution.py
@@ -1,3 +1,4 @@
+import functools
 import math
 import jax
 import jax.numpy as jnp
@@ -5,6 +6,22 @@
 from jax.sharding import PartitionSpec as P
 
 HIGH = lax.Precision.HIGHEST
+
+
+def apply_flows_up(a0, shard_axis, array_dim, out_dim):
+    side_arr = jnp.concatenate(
+        lax.all_to_all(
+            jnp.stack(jnp.split(a0, lax.axis_size(shard_axis), axis=array_dim), axis=0),
+            axis_name=shard_axis,
+            split_axis=0,
+            concat_axis=0,
+        ),
+        axis=out_dim,
+    )
+    return side_arr
+
+
+resolve_the_grid = functools.partial(apply_flows_up, shard_axis="gz", array_dim=1, out_dim=1)
 
 
 def extended(block, sides, width):
@@ -126,7 +143,7 @@
     def reader(updated):
         table = updated.reshape(substrates, highs, lanes)
         looked_up = block_reads(lambda first, count: table, slot_voxel, substrates, highs, lanes)
-        returned = lax.all_to_all(looked_up, "gz", split_axis=1, concat_axis=1, tiled=True)
+        returned = resolve_the_grid(looked_up)
         back = jnp.einsum("pb,spc->sbc", placing, returned, precision=HIGH)
         return back.reshape(substrates, blocks * per_block)
 

time: 119 us -> 107 us (0.90)
  local copies, waits for them, and re-layouts: 17.1 us -> 3.11 us
    dynamic_update_slice x24, local copies, waits for them, and re-layouts: 14.4 us -> 0.32 us  [block_reads(): lax.scan(step, 0, (grouped_vox, jnp.arange(steps_count, dtype=jnp.int32)))]
where the time goes in v1:
time: 107 us; the launch traced here: 106 us
  matrix products  45.4 us (42%)
  starting transfers between devices  27.7 us (26%)
  waiting for transfers between devices  19.2 us (18%)
  other arithmetic  7.86 us (7%)
  local copies, waits for them, and re-layouts  3.11 us (3%)
  loops' own time  2.03 us (2%)
    dot_general x24, matrix products, step(): part = jnp.einsum('gch,qgcl->gqhl', onehot_high, weighted, precision=HIGH)  26.3 us
    dot_general x24, matrix products, step(): picked = jnp.einsum('gch,shl->gscl', onehot_high, table, precision=HIGH)  16.4 us
    ppermute x2, starting transfers between devices, extended(): lax.ppermute(lax.slice_in_dim(block, block.shape[dim] - width, None, axis...  8.46 us
    all_to_all x1, starting transfers between devices, deposit(): lax.all_to_all(send_uptake, 'gz', split_axis=1, concat_axis=1, tiled=True)  6.35 us
    all_to_all x1, waiting for transfers between devices, apply_flows_up(): lax.all_to_all(jnp.stack(jnp.split(a0, lax.axis_size(shard_axis), axis=ar...  5.57 us
    all_to_all x1, waiting for transfers between devices, deposit(): lax.all_to_all(send_index, 'gz', split_axis=1, concat_axis=1, tiled=True)  5.47 us
    all_to_all x1, waiting for transfers between devices, deposit(): lax.all_to_all(send_release, 'gz', split_axis=1, concat_axis=1, tiled=True)  5.03 us
    convert_element_type x48, other arithmetic, one_hots(): ((voxel_group % lanes)[..., None] == lane_ids).astype(jnp.float32)  3.73 us
  transfers between devices with their start and end apart: 8, of which 4 were waited for; matrix products, arithmetic and copies ran while one was open for 3% of the time, Pallas kernels for 0%

profile of v1, /device:TPU:0, one launch (start us, length us, event | category | flops | bytes accessed | tf_op | source)
XLA Modules:
  0.0 106.1 jit_solution(1486302032031391422)
XLA Ops:
  0.6 0.9 convert_reduce_fusion
  2.2 1.2 %convolution_bitcast_fusion = f32[4,96,128]{2,1,0:T(8,128)S(1)} fusion(f32[1,4,32,128]{3,1,2,0:T(4,128)} %bitcast.151, s32[32]{0:T(128)S(1)} %multiply_add_fusion), kind=kOutput, calls=%fused_computation.41 | convolution fusion | flops 18877440 | bytes 262272 | tf_op jit(solution)/shard_map/pb,sbc->spc/dot_general | solution.py:120
  3.4 0.8 copy.20
  4.2 6.3 %all-to-all-start.1 = ((f32[4,96,128]{2,0,1:T(4,128)}), f32[4,96,128]{2,0,1:T(4,128)S(1)}, u32[]{:S(2)}, u32[]{:S(2)}) async-start(f32[4,96,128]{2,0,1:T(4,128)} %copy.20), calls=%async_computation.1 | async-start | bytes 393216 | tf_op jit(solution)/shard_map/all_to_all | solution.py:127
  10.6 3.9 %collective-permute-start.1 = (f32[4,1,8,128]{3,2,1,0:T(8,128)S(1)}, f32[4,1,8,128]{3,2,1,0:T(8,128)S(1)}, u32[]{:S(2)}, u32[]{:S(2)}) collective-permute-start(f32[4,1,8,128]{3,2,1,0:T(8,128)S(1)} %get-tuple-element.160), channel_id=1, source_target_pairs={{0,4},{4,8},{8,12},{1,5},{5,9},{9,13},{2,6},{6,10},{10,14},{3,7},{... | collective-permute-start | bytes 49160 | tf_op jit(solution)/shard_map/ppermute | solution.py:32
  14.5 1.3 %collective-permute-start = (f32[4,1,8,128]{3,2,1,0:T(8,128)S(1)}, f32[4,1,8,128]{3,2,1,0:T(8,128)S(1)}, u32[]{:S(2)}, u32[]{:S(2)}) collective-permute-start(f32[4,1,8,128]{3,2,1,0:T(8,128)S(1)} %get-tuple-element.159), channel_id=1, source_target_pairs={{4,0},{8,4},{12,8},{5,1},{9,5},{13,9},{6,2},{10,6},{14,10},{7,3},{... | collective-permute-start | bytes 49160 | tf_op jit(solution)/shard_map/ppermute | solution.py:35
  16.2 0.8 copy.19
  17.0 3.1 %collective-permute-done = f32[4,1,8,128]{3,2,1,0:T(8,128)S(1)} collective-permute-done((f32[4,1,8,128]{3,2,1,0:T(8,128)S(1)}, f32[4,1,8,128]{3,2,1,0:T(8,128)S(1)}, u32[]{:S(2)}, u32[]{:S(2)}) %collective-permute-start) | collective-permute-done | bytes 16416 | tf_op jit(solution)/shard_map/ppermute | solution.py:35
  20.2 1.3 %collective-permute-start.2 = (f32[4,6,1,128]{3,2,1,0:T(1,128)S(1)}, f32[4,6,1,128]{3,2,1,0:T(1,128)S(1)}, u32[]{:S(2)}, u32[]{:S(2)}) collective-permute-start(f32[4,6,1,128]{3,2,1,0:T(1,128)S(1)} %get-tuple-element.158), channel_id=1, source_target_pairs={{2,0},{3,1},{6,4},{7,5},{10,8},{11,9},{14,12},{15,13},{18,16},{19,... | collective-permute-start | bytes 36872 | tf_op jit(solution)/shard_map/ppermute | solution.py:35
  21.5 4.5 %collective-permute-start.3 = (f32[4,6,1,128]{3,2,1,0:T(1,128)S(1)}, f32[4,6,1,128]{3,2,1,0:T(1,128)S(1)}, u32[]{:S(2)}, u32[]{:S(2)}) collective-permute-start(f32[4,6,1,128]{3,2,1,0:T(1,128)S(1)} %get-tuple-element.157), channel_id=1, source_target_pairs={{0,2},{1,3},{4,6},{5,7},{8,10},{9,11},{12,14},{13,15},{16,18},{17,... | collective-permute-start | bytes 36872 | tf_op jit(solution)/shard_map/ppermute | solution.py:32
  26.0 3.6 %all-to-all-start = ((f32[4,96,128]{2,0,1:T(4,128)}), f32[4,96,128]{2,0,1:T(4,128)S(1)}, u32[]{:S(2)}, u32[]{:S(2)}) async-start(f32[4,96,128]{2,0,1:T(4,128)} %copy.19), calls=%async_computation | async-start | bytes 393216 | tf_op jit(solution)/shard_map/all_to_all | solution.py:126
  29.7 0.9 convolution_convert_fusion
  30.9 5.0 %all-to-all-done = f32[4,96,128]{2,0,1:T(4,128)S(1)} async-done(((f32[4,96,128]{2,0,1:T(4,128)}), f32[4,96,128]{2,0,1:T(4,128)S(1)}, u32[]{:S(2)}, u32[]{:S(2)}) %all-to-all-start) | async-done | bytes 196640 | tf_op jit(solution)/shard_map/all_to_all | solution.py:126
  35.9 3.3 %all-to-all-start.2 = ((s32[1,96,128]{2,0,1:T(1,128)}), s32[1,96,128]{2,0,1:T(1,128)S(1)}, u32[]{:S(2)}, u32[]{:S(2)}) async-start(s32[1,96,128]{2,0,1:T(1,128)} %bitcast.14), calls=%async_computation.2 | async-start | bytes 98304 | tf_op jit(solution)/shard_map/all_to_all | solution.py:128
  39.4 5.5 %all-to-all-done.2 = s32[1,96,128]{2,0,1:T(1,128)S(1)} async-done(((s32[1,96,128]{2,0,1:T(1,128)}), s32[1,96,128]{2,0,1:T(1,128)S(1)}, u32[]{:S(2)}, u32[]{:S(2)}) %all-to-all-start.2) | async-done | bytes 49184 | tf_op jit(solution)/shard_map/all_to_all | solution.py:128
  44.9 31.3 %while.26 = (s32[]{:T(128)}, f32[8,32,128]{2,1,0:T(8,128)S(1)}, f32[24,8,4,128]{3,2,1,0:T(4,128)S(1)}, s32[24,4,128]{2,1,0:T(4,128)S(1)}, s32[]{:T(128)}, /*index=5*/s32[]{:T(128)}) while((s32[]{:T(128)}, f32[8,32,128]{2,1,0:T(8,128)S(1)}, f32[24,8,4,128]{3,2,1,0:T(4,128)S(1)}, s32[24,4,128]{2,1,0:T(4,128)S(1)}, s32[]{:T(128)}, ...), condition=%wide.region_2.3_spmd.clone, body=%wide.region_1.2_spmd.clone.sunk | while | flops 202073600 | bytes 845919 | solution.py:78
  45.1 1.1 %fusion.66 = f32[8,32,128]{2,1,0:T(8,128)S(1)} fusion(f32[4,128,128]{2,1,0:T(8,128)S(1)} %fusion.65, f32[8,4,128]{2,1,0:T(4,128)S(1)} %dynamic-slice_bitcast_fusion.2, f32[8,32,128]{2,1,0:T(8,128)S(1)} %get-tuple-element.226, pred[]{:T(512)S(6)} %compare.42, s32[4,128]{1,0:T(4,128)S(1)} %get-tuple-element.218), kind=kOutput, calls=%fused_computation.22.clone.1 | convolution fusion | flops 201932800 | bytes 542721 | tf_op jit(solution)/shard_map/while/body/eval_jaxpr/gch,qgcl->gqhl/dot_general | solution.py:75
  46.4 1.1 %fusion.66 = f32[8,32,128]{2,1,0:T(8,128)S(1)} fusion(f32[4,128,128]{2,1,0:T(8,128)S(1)} %fusion.65, f32[8,4,128]{2,1,0:T(4,128)S(1)} %dynamic-slice_bitcast_fusion.2, f32[8,32,128]{2,1,0:T(8,128)S(1)} %get-tuple-element.226, pred[]{:T(512)S(6)} %compare.42, s32[4,128]{1,0:T(4,128)S(1)} %get-tuple-element.218), kind=kOutput, calls=%fused_computation.22.clone.1 | convolution fusion | flops 201932800 | bytes 542721 | tf_op jit(solution)/shard_map/while/body/eval_jaxpr/gch,qgcl->gqhl/dot_general | solution.py:75
  47.7 1.1 %fusion.66 = f32[8,32,128]{2,1,0:T(8,128)S(1)} fusion(f32[4,128,128]{2,1,0:T(8,128)S(1)} %fusion.65, f32[8,4,128]{2,1,0:T(4,128)S(1)} %dynamic-slice_bitcast_fusion.2, f32[8,32,128]{2,1,0:T(8,128)S(1)} %get-tuple-element.226, pred[]{:T(512)S(6)} %compare.42, s32[4,128]{1,0:T(4,128)S(1)} %get-tuple-element.218), kind=kOutput, calls=%fused_computation.22.clone.1 | convolution fusion | flops 201932800 | bytes 542721 | tf_op jit(solution)/shard_map/while/body/eval_jaxpr/gch,qgcl->gqhl/dot_general | solution.py:75
  49.0 1.1 %fusion.66 = f32[8,32,128]{2,1,0:T(8,128)S(1)} fusion(f32[4,128,128]{2,1,0:T(8,128)S(1)} %fusion.65, f32[8,4,128]{2,1,0:T(4,128)S(1)} %dynamic-slice_bitcast_fusion.2, f32[8,32,128]{2,1,0:T(8,128)S(1)} %get-tuple-element.226, pred[]{:T(512)S(6)} %compare.42, s32[4,128]{1,0:T(4,128)S(1)} %get-tuple-element.218), kind=kOutput, calls=%fused_computation.22.clone.1 | convolution fusion | flops 201932800 | bytes 542721 | tf_op jit(solution)/shard_map/while/body/eval_jaxpr/gch,qgcl->gqhl/dot_general | solution.py:75
  50.3 1.1 %fusion.66 = f32[8,32,128]{2,1,0:T(8,128)S(1)} fusion(f32[4,128,128]{2,1,0:T(8,128)S(1)} %fusion.65, f32[8,4,128]{2,1,0:T(4,128)S(1)} %dynamic-slice_bitcast_fusion.2, f32[8,32,128]{2,1,0:T(8,128)S(1)} %get-tuple-element.226, pred[]{:T(512)S(6)} %compare.42, s32[4,128]{1,0:T(4,128)S(1)} %get-tuple-element.218), kind=kOutput, calls=%fused_computation.22.clone.1 | convolution fusion | flops 201932800 | bytes 542721 | tf_op jit(solution)/shard_map/while/body/eval_jaxpr/gch,qgcl->gqhl/dot_general | solution.py:75
  51.6 1.1 %fusion.66 = f32[8,32,128]{2,1,0:T(8,128)S(1)} fusion(f32[4,128,128]{2,1,0:T(8,128)S(1)} %fusion.65, f32[8,4,128]{2,1,0:T(4,128)S(1)} %dynamic-slice_bitcast_fusion.2, f32[8,32,128]{2,1,0:T(8,128)S(1)} %get-tuple-element.226, pred[]{:T(512)S(6)} %compare.42, s32[4,128]{1,0:T(4,128)S(1)} %get-tuple-element.218), kind=kOutput, calls=%fused_computation.22.clone.1 | convolution fusion | flops 201932800 | bytes 542721 | tf_op jit(solution)/shard_map/while/body/eval_jaxpr/gch,qgcl->gqhl/dot_general | solution.py:75
  52.9 1.1 %fusion.66 = f32[8,32,128]{2,1,0:T(8,128)S(1)} fusion(f32[4,128,128]{2,1,0:T(8,128)S(1)} %fusion.65, f32[8,4,128]{2,1,0:T(4,128)S(1)} %dynamic-slice_bitcast_fusion.2, f32[8,32,128]{2,1,0:T(8,128)S(1)} %get-tuple-element.226, pred[]{:T(512)S(6)} %compare.42, s32[4,128]{1,0:T(4,128)S(1)} %get-tuple-element.218), kind=kOutput, calls=%fused_computation.22.clone.1 | convolution fusion | flops 201932800 | bytes 542721 | tf_op jit(solution)/shard_map/while/body/eval_jaxpr/gch,qgcl->gqhl/dot_general | solution.py:75
  54.2 1.1 %fusion.66 = f32[8,32,128]{2,1,0:T(8,128)S(1)} fusion(f32[4,128,128]{2,1,0:T(8,128)S(1)} %fusion.65, f32[8,4,128]{2,1,0:T(4,128)S(1)} %dynamic-slice_bitcast_fusion.2, f32[8,32,128]{2,1,0:T(8,128)S(1)} %get-tuple-element.226, pred[]{:T(512)S(6)} %compare.42, s32[4,128]{1,0:T(4,128)S(1)} %get-tuple-element.218), kind=kOutput, calls=%fused_computation.22.clone.1 | convolution fusion | flops 201932800 | bytes 542721 | tf_op jit(solution)/shard_map/while/body/eval_jaxpr/gch,qgcl->gqhl/dot_general | solution.py:75
  55.5 1.1 %fusion.66 = f32[8,32,128]{2,1,0:T(8,128)S(1)} fusion(f32[4,128,128]{2,1,0:T(8,128)S(1)} %fusion.65, f32[8,4,128]{2,1,0:T(4,128)S(1)} %dynamic-slice_bitcast_fusion.2, f32[8,32,128]{2,1,0:T(8,128)S(1)} %get-tuple-element.226, pred[]{:T(512)S(6)} %compare.42, s32[4,128]{1,0:T(4,128)S(1)} %get-tuple-element.218), kind=kOutput, calls=%fused_computation.22.clone.1 | convolution fusion | flops 201932800 | bytes 542721 | tf_op jit(solution)/shard_map/while/body/eval_jaxpr/gch,qgcl->gqhl/dot_general | solution.py:75
  56.8 1.1 %fusion.66 = f32[8,32,128]{2,1,0:T(8,128)S(1)} fusion(f32[4,128,128]{2,1,0:T(8,128)S(1)} %fusion.65, f32[8,4,128]{2,1,0:T(4,128)S(1)} %dynamic-slice_bitcast_fusion.2, f32[8,32,128]{2,1,0:T(8,128)S(1)} %get-tuple-element.226, pred[]{:T(512)S(6)} %compare.42, s32[4,128]{1,0:T(4,128)S(1)} %get-tuple-element.218), kind=kOutput, calls=%fused_computation.22.clone.1 | convolution fusion | flops 201932800 | bytes 542721 | tf_op jit(solution)/shard_map/while/body/eval_jaxpr/gch,qgcl->gqhl/dot_general | solution.py:75
  58.1 1.1 %fusion.66 = f32[8,32,128]{2,1,0:T(8,128)S(1)} fusion(f32[4,128,128]{2,1,0:T(8,128)S(1)} %fusion.65, f32[8,4,128]{2,1,0:T(4,128)S(1)} %dynamic-slice_bitcast_fusion.2, f32[8,32,128]{2,1,0:T(8,128)S(1)} %get-tuple-element.226, pred[]{:T(512)S(6)} %compare.42, s32[4,128]{1,0:T(4,128)S(1)} %get-tuple-element.218), kind=kOutput, calls=%fused_computation.22.clone.1 | convolution fusion | flops 201932800 | bytes 542721 | tf_op jit(solution)/shard_map/while/body/eval_jaxpr/gch,qgcl->gqhl/dot_general | solution.py:75
  59.4 1.1 %fusion.66 = f32[8,32,128]{2,1,0:T(8,128)S(1)} fusion(f32[4,128,128]{2,1,0:T(8,128)S(1)} %fusion.65, f32[8,4,128]{2,1,0:T(4,128)S(1)} %dynamic-slice_bitcast_fusion.2, f32[8,32,128]{2,1,0:T(8,128)S(1)} %get-tuple-element.226, pred[]{:T(512)S(6)} %compare.42, s32[4,128]{1,0:T(4,128)S(1)} %get-tuple-element.218), kind=kOutput, calls=%fused_computation.22.clone.1 | convolution fusion | flops 201932800 | bytes 542721 | tf_op jit(solution)/shard_map/while/body/eval_jaxpr/gch,qgcl->gqhl/dot_general | solution.py:75
  60.7 1.1 %fusion.66 = f32[8,32,128]{2,1,0:T(8,128)S(1)} fusion(f32[4,128,128]{2,1,0:T(8,128)S(1)} %fusion.65, f32[8,4,128]{2,1,0:T(4,128)S(1)} %dynamic-slice_bitcast_fusion.2, f32[8,32,128]{2,1,0:T(8,128)S(1)} %get-tuple-element.226, pred[]{:T(512)S(6)} %compare.42, s32[4,128]{1,0:T(4,128)S(1)} %get-tuple-element.218), kind=kOutput, calls=%fused_computation.22.clone.1 | convolution fusion | flops 201932800 | bytes 542721 | tf_op jit(solution)/shard_map/while/body/eval_jaxpr/gch,qgcl->gqhl/dot_general | solution.py:75
  62.0 1.1 %fusion.66 = f32[8,32,128]{2,1,0:T(8,128)S(1)} fusion(f32[4,128,128]{2,1,0:T(8,128)S(1)} %fusion.65, f32[8,4,128]{2,1,0:T(4,128)S(1)} %dynamic-slice_bitcast_fusion.2, f32[8,32,128]{2,1,0:T(8,128)S(1)} %get-tuple-element.226, pred[]{:T(512)S(6)} %compare.42, s32[4,128]{1,0:T(4,128)S(1)} %get-tuple-element.218), kind=kOutput, calls=%fused_computation.22.clone.1 | convolution fusion | flops 201932800 | bytes 542721 | tf_op jit(solution)/shard_map/while/body/eval_jaxpr/gch,qgcl->gqhl/dot_general | solution.py:75
  63.3 1.1 %fusion.66 = f32[8,32,128]{2,1,0:T(8,128)S(1)} fusion(f32[4,128,128]{2,1,0:T(8,128)S(1)} %fusion.65, f32[8,4,128]{2,1,0:T(4,128)S(1)} %dynamic-slice_bitcast_fusion.2, f32[8,32,128]{2,1,0:T(8,128)S(1)} %get-tuple-element.226, pred[]{:T(512)S(6)} %compare.42, s32[4,128]{1,0:T(4,128)S(1)} %get-tuple-element.218), kind=kOutput, calls=%fused_computation.22.clone.1 | convolution fusion | flops 201932800 | bytes 542721 | tf_op jit(solution)/shard_map/while/body/eval_jaxpr/gch,qgcl->gqhl/dot_general | solution.py:75
  64.6 1.1 %fusion.66 = f32[8,32,128]{2,1,0:T(8,128)S(1)} fusion(f32[4,128,128]{2,1,0:T(8,128)S(1)} %fusion.65, f32[8,4,128]{2,1,0:T(4,128)S(1)} %dynamic-slice_bitcast_fusion.2, f32[8,32,128]{2,1,0:T(8,128)S(1)} %get-tuple-element.226, pred[]{:T(512)S(6)} %compare.42, s32[4,128]{1,0:T(4,128)S(1)} %get-tuple-element.218), kind=kOutput, calls=%fused_computation.22.clone.1 | convolution fusion | flops 201932800 | bytes 542721 | tf_op jit(solution)/shard_map/while/body/eval_jaxpr/gch,qgcl->gqhl/dot_general | solution.py:75
  65.9 1.1 %fusion.66 = f32[8,32,128]{2,1,0:T(8,128)S(1)} fusion(f32[4,128,128]{2,1,0:T(8,128)S(1)} %fusion.65, f32[8,4,128]{2,1,0:T(4,128)S(1)} %dynamic-slice_bitcast_fusion.2, f32[8,32,128]{2,1,0:T(8,128)S(1)} %get-tuple-element.226, pred[]{:T(512)S(6)} %compare.42, s32[4,128]{1,0:T(4,128)S(1)} %get-tuple-element.218), kind=kOutput, calls=%fused_computation.22.clone.1 | convolution fusion | flops 201932800 | bytes 542721 | tf_op jit(solution)/shard_map/while/body/eval_jaxpr/gch,qgcl->gqhl/dot_general | solution.py:75
  67.2 1.1 %fusion.66 = f32[8,32,128]{2,1,0:T(8,128)S(1)} fusion(f32[4,128,128]{2,1,0:T(8,128)S(1)} %fusion.65, f32[8,4,128]{2,1,0:T(4,128)S(1)} %dynamic-slice_bitcast_fusion.2, f32[8,32,128]{2,1,0:T(8,128)S(1)} %get-tuple-element.226, pred[]{:T(512)S(6)} %compare.42, s32[4,128]{1,0:T(4,128)S(1)} %get-tuple-element.218), kind=kOutput, calls=%fused_computation.22.clone.1 | convolution fusion | flops 201932800 | bytes 542721 | tf_op jit(solution)/shard_map/while/body/eval_jaxpr/gch,qgcl->gqhl/dot_general | solution.py:75
  68.5 1.1 %fusion.66 = f32[8,32,128]{2,1,0:T(8,128)S(1)} fusion(f32[4,128,128]{2,1,0:T(8,128)S(1)} %fusion.65, f32[8,4,128]{2,1,0:T(4,128)S(1)} %dynamic-slice_bitcast_fusion.2, f32[8,32,128]{2,1,0:T(8,128)S(1)} %get-tuple-element.226, pred[]{:T(512)S(6)} %compare.42, s32[4,128]{1,0:T(4,128)S(1)} %get-tuple-element.218), kind=kOutput, calls=%fused_computation.22.clone.1 | convolution fusion | flops 201932800 | bytes 542721 | tf_op jit(solution)/shard_map/while/body/eval_jaxpr/gch,qgcl->gqhl/dot_general | solution.py:75
  69.8 1.1 %fusion.66 = f32[8,32,128]{2,1,0:T(8,128)S(1)} fusion(f32[4,128,128]{2,1,0:T(8,128)S(1)} %fusion.65, f32[8,4,128]{2,1,0:T(4,128)S(1)} %dynamic-slice_bitcast_fusion.2, f32[8,32,128]{2,1,0:T(8,128)S(1)} %get-tuple-element.226, pred[]{:T(512)S(6)} %compare.42, s32[4,128]{1,0:T(4,128)S(1)} %get-tuple-element.218), kind=kOutput, calls=%fused_computation.22.clone.1 | convolution fusion | flops 201932800 | bytes 542721 | tf_op jit(solution)/shard_map/while/body/eval_jaxpr/gch,qgcl->gqhl/dot_general | solution.py:75
  71.1 1.1 %fusion.66 = f32[8,32,128]{2,1,0:T(8,128)S(1)} fusion(f32[4,128,128]{2,1,0:T(8,128)S(1)} %fusion.65, f32[8,4,128]{2,1,0:T(4,128)S(1)} %dynamic-slice_bitcast_fusion.2, f32[8,32,128]{2,1,0:T(8,128)S(1)} %get-tuple-element.226, pred[]{:T(512)S(6)} %compare.42, s32[4,128]{1,0:T(4,128)S(1)} %get-tuple-element.218), kind=kOutput, calls=%fused_computation.22.clone.1 | convolution fusion | flops 201932800 | bytes 542721 | tf_op jit(solution)/shard_map/while/body/eval_jaxpr/gch,qgcl->gqhl/dot_general | solution.py:75
  72.4 1.1 %fusion.66 = f32[8,32,128]{2,1,0:T(8,128)S(1)} fusion(f32[4,128,128]{2,1,0:T(8,128)S(1)} %fusion.65, f32[8,4,128]{2,1,0:T(4,128)S(1)} %dynamic-slice_bitcast_fusion.2, f32[8,32,128]{2,1,0:T(8,128)S(1)} %get-tuple-element.226, pred[]{:T(512)S(6)} %compare.42, s32[4,128]{1,0:T(4,128)S(1)} %get-tuple-element.218), kind=kOutput, calls=%fused_computation.22.clone.1 | convolution fusion | flops 201932800 | bytes 542721 | tf_op jit(solution)/shard_map/while/body/eval_jaxpr/gch,qgcl->gqhl/dot_general | solution.py:75
  73.7 1.1 %fusion.66 = f32[8,32,128]{2,1,0:T(8,128)S(1)} fusion(f32[4,128,128]{2,1,0:T(8,128)S(1)} %fusion.65, f32[8,4,128]{2,1,0:T(4,128)S(1)} %dynamic-slice_bitcast_fusion.2, f32[8,32,128]{2,1,0:T(8,128)S(1)} %get-tuple-element.226, pred[]{:T(512)S(6)} %compare.42, s32[4,128]{1,0:T(4,128)S(1)} %get-tuple-element.218), kind=kOutput, calls=%fused_computation.22.clone.1 | convolution fusion | flops 201932800 | bytes 542721 | tf_op jit(solution)/shard_map/while/body/eval_jaxpr/gch,qgcl->gqhl/dot_general | solution.py:75
  75.0 1.1 %fusion.66 = f32[8,32,128]{2,1,0:T(8,128)S(1)} fusion(f32[4,128,128]{2,1,0:T(8,128)S(1)} %fusion.65, f32[8,4,128]{2,1,0:T(4,128)S(1)} %dynamic-slice_bitcast_fusion.2, f32[8,32,128]{2,1,0:T(8,128)S(1)} %get-tuple-element.226, pred[]{:T(512)S(6)} %compare.42, s32[4,128]{1,0:T(4,128)S(1)} %get-tuple-element.218), kind=kOutput, calls=%fused_computation.22.clone.1 | convolution fusion | flops 201932800 | bytes 542721 | tf_op jit(solution)/shard_map/while/body/eval_jaxpr/gch,qgcl->gqhl/dot_general | solution.py:75
  76.3 18.5 %while.25 = (s32[]{:T(128)}, f32[24,4,4,128]{3,2,1,0:T(4,128)S(1)}, s32[24,4,128]{2,1,0:T(4,128)S(1)}, f32[4,32,128]{2,1,0:T(8,128)S(1)}, s32[]{:T(128)}) while((s32[]{:T(128)}, f32[24,4,4,128]{3,2,1,0:T(4,128)S(1)}, s32[24,4,128]{2,1,0:T(4,128)S(1)}, f32[4,32,128]{2,1,0:T(8,128)S(1)}, s32[]{:T(128)}) %tuple.75), condition=%wide.region_5.6_spmd, body=%wide.region_3.5_spmd.sunk | while | flops 101342720 | bytes 624717 | solution.py:97
  76.3 0.7 fusion.62
  77.9 0.7 fusion.62
  78.7 0.7 fusion.62
  79.4 0.7 fusion.62
  80.2 0.7 fusion.62
  81.0 0.7 fusion.62
  81.7 0.7 fusion.62
  82.5 0.7 fusion.62
  83.3 0.7 fusion.62
  84.0 0.7 fusion.62
  84.8 0.7 fusion.62
  85.6 0.7 fusion.62
  86.4 0.7 fusion.62
  87.1 0.7 fusion.62
  87.9 0.7 fusion.62
  88.7 0.7 fusion.62
  90.2 0.7 fusion.62
  91.7 0.7 fusion.62
  93.3 0.7 fusion.62
  94.1 0.7 fusion.62
  94.9 0.7 pad_maximum_fusion.1
  95.6 3.4 %all-to-all-start.3 = ((f32[4,4,24,128]{3,2,1,0:T(8,128)}), f32[4,4,24,128]{3,2,1,0:T(8,128)S(1)}, u32[]{:S(2)}, u32[]{:S(2)}) async-start(f32[4,4,24,128]{3,2,1,0:T(8,128)} %pad_maximum_fusion.1), calls=%async_computation.3 | async-start | bytes 393216 | tf_op jit(solution)/shard_map/all_to_all | solution.py:13
  99.6 5.6 %all-to-all-done.3 = f32[4,4,24,128]{3,2,1,0:T(8,128)S(1)} async-done(((f32[4,4,24,128]{3,2,1,0:T(8,128)}), f32[4,4,24,128]{3,2,1,0:T(8,128)S(1)}, u32[]{:S(2)}, u32[]{:S(2)}) %all-to-all-start.3) | async-done | bytes 196640 | tf_op jit(solution)/shard_map/all_to_all | solution.py:13
  (179 shorter events, 11.0 us)
Async XLA Ops:
  3.4 7.2 %copy-start = (f32[4,4,8,128]{3,2,1,0:T(8,128)S(1)}, f32[4,4,8,128]{3,2,1,0:T(8,128)}, u32[]{:S(2)}) copy-start(f32[4,4,8,128]{3,2,1,0:T(8,128)} %param.10) | copy-start | bytes 196612
  3.4 12.4 %copy-start.1 = (f32[4,4096]{1,0:T(4,128)S(1)}, f32[4,4096]{1,0:T(4,128)}, u32[]{:S(2)}) copy-start(f32[4,4096]{1,0:T(4,128)} %param.12) | copy-start | bytes 196612
  4.2 21.8 %all-to-all-start.1 = ((f32[4,96,128]{2,0,1:T(4,128)}), f32[4,96,128]{2,0,1:T(4,128)S(1)}, u32[]{:S(2)}, u32[]{:S(2)}) async-start(f32[4,96,128]{2,0,1:T(4,128)} %copy.20), calls=%async_computation.1 | async-start | bytes 393216 | tf_op jit(solution)/shard_map/all_to_all | solution.py:127
  10.6 6.4 %collective-permute-start.1 = (f32[4,1,8,128]{3,2,1,0:T(8,128)S(1)}, f32[4,1,8,128]{3,2,1,0:T(8,128)S(1)}, u32[]{:S(2)}, u32[]{:S(2)}) collective-permute-start(f32[4,1,8,128]{3,2,1,0:T(8,128)S(1)} %get-tuple-element.160), channel_id=1, source_target_pairs={{0,4},{4,8},{8,12},{1,5},{5,9},{9,13},{2,6},{6,10},{10,14},{3,7},{... | collective-permute-start | bytes 49160 | tf_op jit(solution)/shard_map/ppermute | solution.py:32
  14.5 5.6 %collective-permute-start = (f32[4,1,8,128]{3,2,1,0:T(8,128)S(1)}, f32[4,1,8,128]{3,2,1,0:T(8,128)S(1)}, u32[]{:S(2)}, u32[]{:S(2)}) collective-permute-start(f32[4,1,8,128]{3,2,1,0:T(8,128)S(1)} %get-tuple-element.159), channel_id=1, source_target_pairs={{4,0},{8,4},{12,8},{5,1},{9,5},{13,9},{6,2},{10,6},{14,10},{7,3},{... | collective-permute-start | bytes 49160 | tf_op jit(solution)/shard_map/ppermute | solution.py:35
  17.0 12.7 %copy-start.2 = (s32[4096]{0:T(1024)S(1)}, s32[4096]{0:T(1024)}, u32[]{:S(2)}) copy-start(s32[4096]{0:T(1024)} %param.14) | copy-start | bytes 49156
  20.2 10.4 %collective-permute-start.2 = (f32[4,6,1,128]{3,2,1,0:T(1,128)S(1)}, f32[4,6,1,128]{3,2,1,0:T(1,128)S(1)}, u32[]{:S(2)}, u32[]{:S(2)}) collective-permute-start(f32[4,6,1,128]{3,2,1,0:T(1,128)S(1)} %get-tuple-element.158), channel_id=1, source_target_pairs={{2,0},{3,1},{6,4},{7,5},{10,8},{11,9},{14,12},{15,13},{18,16},{19,... | collective-permute-start | bytes 36872 | tf_op jit(solution)/shard_map/ppermute | solution.py:35
  21.5 9.1 %collective-permute-start.3 = (f32[4,6,1,128]{3,2,1,0:T(1,128)S(1)}, f32[4,6,1,128]{3,2,1,0:T(1,128)S(1)}, u32[]{:S(2)}, u32[]{:S(2)}) collective-permute-start(f32[4,6,1,128]{3,2,1,0:T(1,128)S(1)} %get-tuple-element.157), channel_id=1, source_target_pairs={{0,2},{1,3},{4,6},{5,7},{8,10},{9,11},{12,14},{13,15},{16,18},{17,... | collective-permute-start | bytes 36872 | tf_op jit(solution)/shard_map/ppermute | solution.py:32
  26.0 9.9 %all-to-all-start = ((f32[4,96,128]{2,0,1:T(4,128)}), f32[4,96,128]{2,0,1:T(4,128)S(1)}, u32[]{:S(2)}, u32[]{:S(2)}) async-start(f32[4,96,128]{2,0,1:T(4,128)} %copy.19), calls=%async_computation | async-start | bytes 393216 | tf_op jit(solution)/shard_map/all_to_all | solution.py:126
  35.9 8.9 %all-to-all-start.2 = ((s32[1,96,128]{2,0,1:T(1,128)}), s32[1,96,128]{2,0,1:T(1,128)S(1)}, u32[]{:S(2)}, u32[]{:S(2)}) async-start(s32[1,96,128]{2,0,1:T(1,128)} %bitcast.14), calls=%async_computation.2 | async-start | bytes 98304 | tf_op jit(solution)/shard_map/all_to_all | solution.py:128
  44.9 31.3 %copy-start.3 = (f32[4]{0:T(128)S(1)}, f32[4]{0:T(128)}, u32[]{:S(2)}) copy-start(f32[4]{0:T(128)} %param.11) | copy-start | bytes 52
  95.6 9.6 %all-to-all-start.3 = ((f32[4,4,24,128]{3,2,1,0:T(8,128)}), f32[4,4,24,128]{3,2,1,0:T(8,128)S(1)}, u32[]{:S(2)}, u32[]{:S(2)}) async-start(f32[4,4,24,128]{3,2,1,0:T(8,128)} %pad_maximum_fusion.1), calls=%async_computation.3 | async-start | bytes 393216 | tf_op jit(solution)/shard_map/all_to_all | solution.py:13
